TPU v7x, 32 devices: a whole 2x2x4 slice. The times are simulated.
32 devices in a mesh: items: 16 (over z, y, core), seq: 2 (over x).
Axes of the slice: x: 2, y: 2, z: 4, core: 2. Of those that a mesh axis runs over, the one named last changes fastest.
Arguments:
- frames: bfloat16 [16, 1280, 1024], P('items', 'seq'), may hold values from -6 to 6
- cotangent: bfloat16 [16, 1280, 1024], P('items', 'seq'), may hold values from -6 to 6
- section: int32 [16], P('items'), may hold values from 0 to 7
- prompt_len: int32 [16], P('items'), may hold values from 150 to 600, as said below
- section_embed: float32 [8, 1024], replicated, may hold values from -6 to 6
- ada_proj: bfloat16 [1024, 4096], replicated, may hold values from -0.09375 to 0.09375
- ada_bias: float32 [4096], replicated, may hold values from -4 to 4
- w_qkv: bfloat16 [1024, 3072], replicated, may hold values from -0.1875 to 0.1875
- w_out: bfloat16 [1024, 1024], replicated, may hold values from -3.5 to 3.5
- w_up: bfloat16 [1024, 4096], replicated, may hold values from -0.1875 to 0.1875
- w_down: bfloat16 [4096, 1024], replicated, may hold values from -0.125 to 0.125
Outputs:
- out_frames: bfloat16 [16, 1280, 1024], P('items', 'seq')
- frames_grad: bfloat16 [16, 1280, 1024], P('items', 'seq')
- section_embed_grad: float32 [8, 1024], P(None, 'items')
- ada_proj_grad: float32 [1024, 4096], P('items')
- ada_bias_grad: float32 [4096], P('items')
- w_qkv_grad: float32 [1024, 3072], P('items')
- w_out_grad: float32 [1024, 1024], P('items')
- w_up_grad: float32 [1024, 4096], P('items')
- w_down_grad: float32 [4096, 1024], P('items')
Inputs may be any that keep to these rules, and one draw needn't show every extreme that they name: `prompt_len`: some item has exactly 600 prompt frames.
All inputs are finite; a program needn't handle non-finite values.
Results may differ from a plain program's by a relative error of at most 0.018.
Values may be sent and summed in bfloat16 or wider, within the bound.
A program may use at most 640 MiB of HBM per device.

v0:
```python
import jax
import jax.numpy as jnp
from jax import lax
from jax.sharding import PartitionSpec as P

HEADS = 16
EPS = 1e-05
NEGATIVE = -1e30
SQRT_HALF = 0.7071067811865476
INV_SQRT_TAU = 0.3989422804014327
HIGHEST = lax.Precision.HIGHEST


def normalize(values):
    mean = jnp.mean(values, -1, keepdims=True)
    centered = values - mean
    inverse = lax.rsqrt(jnp.mean(centered * centered, -1, keepdims=True) + EPS)
    return (centered * inverse, inverse)


def norm_back(grad, normed, inverse):
    first = jnp.mean(grad, -1, keepdims=True)
    second = jnp.mean(grad * normed, -1, keepdims=True)
    return (grad - first - normed * second) * inverse


def gelu_exact(values):
    return 0.5 * values * (1.0 + lax.erf(values * SQRT_HALF))


def gelu_slope(values):
    return (
        0.5 * (1.0 + lax.erf(values * SQRT_HALF))
        + values * jnp.exp(-0.5 * values * values) * INV_SQRT_TAU
    )


def project(left, weight):
    flat = left.reshape(-1, left.shape[-1])
    result = jnp.dot(flat, weight, preferred_element_type=jnp.float32)
    return result.reshape(left.shape[:-1] + (weight.shape[1],))


def back_project(grad, weight):
    flat = grad.reshape(-1, grad.shape[-1])
    result = lax.dot_general(
        flat, weight, (((1,), (1,)), ((), ())), preferred_element_type=jnp.float32
    )
    return result.reshape(grad.shape[:-1] + (weight.shape[0],))


def outer_sum(left, right):
    left_flat = left.reshape(-1, left.shape[-1])
    right_flat = right.reshape(-1, right.shape[-1])
    return lax.dot_general(
        left_flat, right_flat, (((0,), (0,)), ((), ())), preferred_element_type=jnp.float32
    )


def per_device(
    frames,
    cotangent,
    section,
    prompt_len,
    section_embed,
    ada_proj,
    ada_bias,
    w_qkv,
    w_out,
    w_up,
    w_down,
):
    group_count, row_count, width = frames.shape
    head_count = HEADS
    head_size = width // head_count
    scale = head_size ** (-0.5)
    section_count = section_embed.shape[0]
    onehot = (section[:, None] == jnp.arange(section_count, dtype=jnp.int32)[None, :]).astype(
        jnp.float32
    )
    cond = jnp.dot(onehot, section_embed, precision=HIGHEST)
    ada_full = ada_proj.astype(jnp.float32)
    modul = jnp.dot(cond, ada_full, precision=HIGHEST) + ada_bias[None, :]
    scale_one, shift_one, scale_two, shift_two = jnp.split(modul, 4, axis=-1)
    inputs = frames.astype(jnp.float32)
    normed_one, inv_one = normalize(inputs)
    attn_in = (normed_one * (1.0 + scale_one[:, None, :]) + shift_one[:, None, :]).astype(
        jnp.bfloat16
    )
    qkv = project(attn_in, w_qkv)
    query = qkv[..., :width].astype(jnp.bfloat16)
    key_local = qkv[..., width : 2 * width].astype(jnp.bfloat16)
    value_local = qkv[..., 2 * width :].astype(jnp.bfloat16)
    query_heads = query.reshape(group_count, row_count, head_count, head_size)

    def key_mask(count):
        position = jnp.arange(count, dtype=jnp.int32)
        valid = (position[None, :] >= row_count) | (position[None, :] < prompt_len[:, None])
        return valid[:, None, None, :]

    run_max = jnp.full((group_count, head_count, row_count), NEGATIVE, jnp.float32)
    key_piece = lax.all_gather(key_local, "seq", axis=1, tiled=True)
    value_piece = lax.all_gather(value_local, "seq", axis=1, tiled=True)
    count = key_piece.shape[1]
    key_heads = key_piece.reshape(group_count, count, head_count, head_size)
    value_heads = value_piece.reshape(group_count, count, head_count, head_size)
    valid = key_mask(count)
    scores = (
        jnp.einsum("grhd,gkhd->ghrk", query_heads, key_heads, preferred_element_type=jnp.float32)
        * scale
    )
    scores = jnp.where(valid, scores, NEGATIVE)
    new_max = jnp.maximum(run_max, jnp.max(scores, -1))
    weights = jnp.where(valid, jnp.exp(scores - new_max[..., None]), 0.0)
    new_sum = jnp.sum(weights, -1)
    update = jnp.einsum(
        "ghrk,gkhd->grhd",
        weights.astype(jnp.bfloat16),
        value_heads,
        preferred_element_type=jnp.float32,
    )
    accum = update
    run_max, run_sum, accum = (new_max, new_sum, accum)
    att_heads = accum / jnp.transpose(run_sum, (0, 2, 1))[..., None]
    log_total = run_max + jnp.log(run_sum)
    att = att_heads.reshape(group_count, row_count, width).astype(jnp.bfloat16)
    mid = inputs + project(att, w_out)
    normed_two, inv_two = normalize(mid)
    ffn_in = (normed_two * (1.0 + scale_two[:, None, :]) + shift_two[:, None, :]).astype(
        jnp.bfloat16
    )
    upper = project(ffn_in, w_up)
    act = gelu_exact(upper).astype(jnp.bfloat16)
    out_frames = (mid + project(act, w_down)).astype(jnp.bfloat16)
    grad_out = cotangent.astype(jnp.float32)
    grad_w_down = outer_sum(act, cotangent)
    grad_upper = (back_project(cotangent, w_down) * gelu_slope(upper)).astype(jnp.bfloat16)
    grad_w_up = outer_sum(ffn_in, grad_upper)
    grad_ffn_in = back_project(grad_upper, w_up)
    grad_scale_two = jnp.sum(grad_ffn_in * normed_two, 1)
    grad_shift_two = jnp.sum(grad_ffn_in, 1)
    grad_mid = grad_out + norm_back(
        grad_ffn_in * (1.0 + scale_two[:, None, :]), normed_two, inv_two
    )
    grad_mid_low = grad_mid.astype(jnp.bfloat16)
    grad_w_out = outer_sum(att, grad_mid_low)
    grad_att = back_project(grad_mid_low, w_out).astype(jnp.bfloat16)
    grad_att_heads = grad_att.reshape(group_count, row_count, head_count, head_size)
    delta = jnp.transpose(jnp.sum(grad_att_heads.astype(jnp.float32) * att_heads, -1), (0, 2, 1))
    key_piece = lax.all_gather(key_local, "seq", axis=1, tiled=True)
    value_piece = lax.all_gather(value_local, "seq", axis=1, tiled=True)
    count = key_piece.shape[1]
    key_heads = key_piece.reshape(group_count, count, head_count, head_size)
    value_heads = value_piece.reshape(group_count, count, head_count, head_size)
    valid = key_mask(count)
    scores = (
        jnp.einsum("grhd,gkhd->ghrk", query_heads, key_heads, preferred_element_type=jnp.float32)
        * scale
    )
    probs = jnp.where(valid, jnp.exp(scores - log_total[..., None]), 0.0)
    value_part = jnp.einsum(
        "ghrk,grhd->gkhd",
        probs.astype(jnp.bfloat16),
        grad_att_heads,
        preferred_element_type=jnp.float32,
    )
    grad_probs = jnp.einsum(
        "grhd,gkhd->ghrk", grad_att_heads, value_heads, preferred_element_type=jnp.float32
    )
    grad_scores = (probs * (grad_probs - delta[..., None])).astype(jnp.bfloat16)
    grad_query = (
        jnp.einsum("ghrk,gkhd->grhd", grad_scores, key_heads, preferred_element_type=jnp.float32)
        * scale
    )
    key_part = (
        jnp.einsum("ghrk,grhd->gkhd", grad_scores, query_heads, preferred_element_type=jnp.float32)
        * scale
    )
    grad_keys = key_part.reshape(group_count, count, width)
    grad_values = value_part.reshape(group_count, count, width)
    back_result = (grad_query, grad_keys, grad_values)
    grad_query, grad_keys, grad_values = back_result
    own_keys, own_values = (
        lax.psum_scatter(
            grad_keys.astype(jnp.bfloat16), "seq", scatter_dimension=1, tiled=True
        ).astype(jnp.float32),
        lax.psum_scatter(
            grad_values.astype(jnp.bfloat16), "seq", scatter_dimension=1, tiled=True
        ).astype(jnp.float32),
    )
    grad_qkv = jnp.concatenate(
        [
            grad_query.reshape(group_count, row_count, width).astype(jnp.bfloat16),
            own_keys.astype(jnp.bfloat16),
            own_values.astype(jnp.bfloat16),
        ],
        -1,
    )
    grad_w_qkv = outer_sum(attn_in, grad_qkv)
    grad_attn_in = back_project(grad_qkv, w_qkv)
    grad_scale_one = jnp.sum(grad_attn_in * normed_one, 1)
    grad_shift_one = jnp.sum(grad_attn_in, 1)
    frames_grad = (
        grad_mid + norm_back(grad_attn_in * (1.0 + scale_one[:, None, :]), normed_one, inv_one)
    ).astype(jnp.bfloat16)
    grad_modul = jnp.concatenate(
        [grad_scale_one, grad_shift_one, grad_scale_two, grad_shift_two], -1
    )
    grad_ada = lax.dot_general(cond, grad_modul, (((0,), (0,)), ((), ())), precision=HIGHEST)
    grad_bias = jnp.sum(grad_modul, 0)
    grad_cond = lax.dot_general(grad_modul, ada_full, (((1,), (1,)), ((), ())), precision=HIGHEST)
    grad_embed = lax.dot_general(onehot, grad_cond, (((0,), (0,)), ((), ())), precision=HIGHEST)
    parts = (
        lax.psum_scatter(
            grad_embed.astype(jnp.bfloat16), "items", scatter_dimension=1, tiled=True
        ).astype(jnp.float32),
        lax.psum_scatter(
            grad_ada.astype(jnp.bfloat16), "items", scatter_dimension=0, tiled=True
        ).astype(jnp.float32),
        lax.psum_scatter(
            grad_bias.astype(jnp.bfloat16), "items", scatter_dimension=0, tiled=True
        ).astype(jnp.float32),
        lax.psum_scatter(
            grad_w_qkv.astype(jnp.bfloat16), "items", scatter_dimension=0, tiled=True
        ).astype(jnp.float32),
        lax.psum_scatter(
            grad_w_out.astype(jnp.bfloat16), "items", scatter_dimension=0, tiled=True
        ).astype(jnp.float32),
        lax.psum_scatter(
            grad_w_up.astype(jnp.bfloat16), "items", scatter_dimension=0, tiled=True
        ).astype(jnp.float32),
        lax.psum_scatter(
            grad_w_down.astype(jnp.bfloat16), "items", scatter_dimension=0, tiled=True
        ).astype(jnp.float32),
    )
    sum_embed, sum_ada, sum_bias, sum_qkv, sum_out, sum_up, sum_down = (
        lax.psum(parts[0].astype(jnp.bfloat16), "seq").astype(jnp.float32),
        lax.psum(parts[1].astype(jnp.bfloat16), "seq").astype(jnp.float32),
        lax.psum(parts[2].astype(jnp.bfloat16), "seq").astype(jnp.float32),
        lax.psum(parts[3].astype(jnp.bfloat16), "seq").astype(jnp.float32),
        lax.psum(parts[4].astype(jnp.bfloat16), "seq").astype(jnp.float32),
        lax.psum(parts[5].astype(jnp.bfloat16), "seq").astype(jnp.float32),
        lax.psum(parts[6].astype(jnp.bfloat16), "seq").astype(jnp.float32),
    )
    return (
        out_frames,
        frames_grad,
        sum_embed,
        sum_ada,
        sum_bias,
        sum_qkv,
        sum_out,
        sum_up,
        sum_down,
    )


def solution(mesh):
    in_specs = (
        P("items", "seq", None),
        P("items", "seq", None),
        P("items"),
        P("items"),
        P(),
        P(),
        P(),
        P(),
        P(),
        P(),
        P(),
    )
    out_specs = (
        P("items", "seq", None),
        P("items", "seq", None),
        P(None, "items"),
        P("items", None),
        P("items"),
        P("items", None),
        P("items", None),
        P("items", None),
        P("items", None),
    )
    return jax.shard_map(
        per_device, mesh=mesh, in_specs=in_specs, out_specs=out_specs, check_vma=False
    )
```

profile of v0, /device:TPU:0, one launch (start us, length us, event | category | flops | bytes accessed | tf_op | source)
XLA Modules:
  0.0 937.2 jit_solution(6268356600912304803)
XLA Ops:
  28.3 38.2 %all-gather.5.cloned.1.call-done = bf16[1,1280,1024]{2,1,0:T(8,128)(2,1)} async-done(((bf16[1,640,1024]{2,1,0:T(8,128)(2,1)}), bf16[1,1280,1024]{2,1,0:T(8,128)(2,1)}) %all-gather.5.cloned.1.call-update) | async-done | bytes 2621456 | tf_op jit(solution)/shard_map/all_gather | solution.py:102
  71.0 20.5 %select_reduce_fusion = (f32[16,640]{1,0:T(8,128)S(1)}, f32[16,640,1280]{2,1,0:T(8,128)}) fusion(pred[1280]{0:T(1024)(128)(4,1)S(1)} %fusion.52, bf16[640,16,64]{0,2,1:T(8,128)(2,1)S(1)} %bitcast.164, bf16[1280,16,64]{0,2,1:T(8,128)(2,1)} %bitcast.160), kind=kOutput, calls=%fused_computation.3 | convolution fusion | flops 1717032960 | bytes 56403200 | tf_op jit(solution)/shard_map/grhd,gkhd->ghrk/dot_general | solution.py:109
  91.5 17.1 %fusion.1 = f32[16,640]{1,0:T(8,128)S(1)} fusion(f32[16,640,1280]{2,1,0:T(8,128)} %get-tuple-element.32, f32[16,640]{1,0:T(8,128)S(1)} %broadcast_maximum_fusion, pred[1280]{0:T(1024)(128)(4,1)S(1)} %fusion.52), kind=kLoop, calls=%fused_computation.5 | loop fusion | flops 65525760 | bytes 52512000 | tf_op jit(solution)/shard_map/reduce_sum | solution.py:115
  113.0 22.3 %fusion.75 = (bf16[1,640,16,64]{1,3,2,0:T(8,128)(2,1)S(1)}, f32[1,640,16,64]{1,3,2,0:T(8,128)}) fusion(f32[640,16]{0,1:T(8,128)S(1)} %bitcast.178, bf16[1280,16,64]{0,2,1:T(8,128)(2,1)} %bitcast.170, f32[16,640,1280]{2,1,0:T(8,128)} %get-tuple-element.32, f32[16,640]{1,0:T(8,128)S(1)} %broadcast_maximum_fusion, pred[1280]{0:T(1024)(128)(4,1)S(1)} %fusion.52), kind=kOutput, calls=%fused_computation.117 | convolution fusion | flops 1744568320 | bytes 59065600 | tf_op jit(solution)/shard_map/ghrk,gkhd->grhd/dot_general | solution.py:116
  137.4 12.4 %multiply_convert_fusion.2 = (bf16[640,4096]{1,0:T(8,128)(2,1)}, f32[640,4096]{1,0:T(8,128)}) fusion(bf16[1024,4096]{1,0:T(8,128)(2,1)} %param.20, f32[1,640,1024]{2,1,0:T(8,128)S(1)} %get-tuple-element.36, f32[1024]{0:T(1024)S(1)} %bitcast.207, f32[1024]{0:T(1024)S(1)} %bitcast.192, f32[640]{0:T(1024)S(1)} %add_rsqrt_fusion, ...), kind=kOutput, calls=%fused_computation.19 | convolution fusion | flops 5385093120 | bytes 26752000 | tf_op jit(solution)/shard_map/dot_general | solution.py:40
  149.8 14.0 %fusion.14 = bf16[640,4096]{1,0:T(8,128)(2,1)} fusion(f32[640,4096]{1,0:T(8,128)} %get-tuple-element.38, bf16[4096,1024]{1,0:T(8,128)(2,1)} %param.21, bf16[1,640,1024]{2,1,0:T(8,128)(2,1)S(1)} %copy-done.13), kind=kOutput, calls=%fused_computation.18 | convolution fusion | flops 5394923520 | bytes 25427968 | tf_op jit(solution)/shard_map/dot_general | solution.py:46
  179.4 21.4 %fusion.16 = bf16[16,64,1280]{2,1,0:T(8,128)(2,1)} fusion(bf16[640,16,64]{0,2,1:T(8,128)(2,1)S(1)} %bitcast.175, f32[16,640,1280]{2,1,0:T(8,128)} %get-tuple-element.32, f32[16,640]{1,0:T(8,128)S(1)} %log_add_fusion, pred[1280]{0:T(1024)(128)(4,1)S(1)} %fusion.52), kind=kOutput, calls=%fused_computation.31 | convolution fusion | flops 1731461120 | bytes 56403200 | tf_op jit(solution)/shard_map/ghrk,grhd->gkhd/dot_general | solution.py:161
  200.8 11.5 %copy.41 = bf16[1,1280,1024]{2,0,1:T(2,128)(2,1)} copy(bf16[1,1280,1024]{1,2,0:T(8,128)(2,1)} %bitcast.172) | data formatting | bytes 5242880
  221.2 33.9 %multiply_convert_fusion = bf16[16,640,1280]{2,1,0:T(8,128)(2,1)} fusion(f32[16,640,1280]{2,1,0:T(8,128)} %get-tuple-element.32, bf16[640,16,64]{0,2,1:T(8,128)(2,1)S(1)} %bitcast.176, bf16[1280,16,64]{0,2,1:T(8,128)(2,1)S(1)} %bitcast.171, f32[16,640]{1,0:T(8,128)S(1)} %bitcast.184, f32[16,640]{1,0:T(8,128)S(1)} %log_add_fusion, pred[1280]{0:T(1024)(128)(4,1)S(1)} %fusion.52), kind=kOutput, calls=%fused_computation | convolution fusion | flops 1756364800 | bytes 82658560 | tf_op jit(solution)/shard_map/grhd,gkhd->ghrk/dot_general | solution.py:167
  255.0 14.6 %multiply_convert_fusion.3 = bf16[16,64,1280]{2,1,0:T(8,128)(2,1)} fusion(bf16[640,16,64]{0,2,1:T(8,128)(2,1)S(1)} %bitcast.165, bf16[16,640,1280]{2,1,0:T(8,128)(2,1)} %multiply_convert_fusion), kind=kOutput, calls=%fused_computation.24 | convolution fusion | flops 1680343040 | bytes 30146560 | tf_op jit(solution)/shard_map/ghrk,grhd->gkhd/dot_general | solution.py:176
  269.6 11.6 %copy.39 = bf16[1,1280,1024]{2,0,1:T(2,128)(2,1)} copy(bf16[1,1280,1024]{1,2,0:T(8,128)(2,1)} %bitcast.166) | data formatting | bytes 5242880
  292.5 12.2 %convolution_convert_fusion = bf16[1024,4096]{1,0:T(8,128)(2,1)} fusion(bf16[640,4096]{1,0:T(8,128)(2,1)} %fusion.14, f32[1,640,1024]{2,1,0:T(8,128)} %copy-done.9, f32[1024]{0:T(1024)S(1)} %bitcast.208, f32[1024]{0:T(1024)S(1)} %bitcast.196, f32[640]{0:T(1024)S(1)} %add_rsqrt_fusion, f32[640]{0:T(1024)S(1)} %broadcast_multiply_fusion.4), kind=kOutput, calls=%fused_computation.21 | convolution fusion | flops 5376180224 | bytes 16266240 | tf_op jit(solution)/shard_map/dot_general | solution.py:55
  306.0 11.5 %convolution_convert_fusion.1 = bf16[4096,1024]{1,0:T(8,128)(2,1)} fusion(bf16[640,4096]{1,0:T(8,128)(2,1)} %get-tuple-element.37, bf16[1,640,1024]{2,1,0:T(8,128)(2,1)S(1)} %copy-done.14), kind=kOutput, calls=%fused_computation.22 | convolution fusion | flops 5372903424 | bytes 14942208 | tf_op jit(solution)/shard_map/dot_general | solution.py:55
  317.7 13.9 %multiply_convert_fusion.4 = bf16[16,64,640]{2,1,0:T(8,128)(2,1)S(1)} fusion(bf16[1280,16,64]{0,2,1:T(8,128)(2,1)} %bitcast.161, bf16[16,640,1280]{2,1,0:T(8,128)(2,1)} %multiply_convert_fusion), kind=kOutput, calls=%fused_computation.61 | convolution fusion | flops 1679032320 | bytes 30146560 | tf_op jit(solution)/shard_map/ghrk,gkhd->grhd/dot_general | solution.py:172
  352.5 9.9 %convolution_convert_fusion.2 = bf16[1024,3072]{1,0:T(8,128)(2,1)} fusion(bf16[1,640,1024]{1,2,0:T(8,128)(2,1)} %copy.42, bf16[1,640,1024]{1,2,0:T(8,128)(2,1)} %copy.40, bf16[1,640,1024]{1,2,0:T(8,128)(2,1)S(1)} %bitcast.173, bf16[1,640,1024]{2,1,0:T(8,128)(2,1)S(1)} %copy-done.6, f32[1024]{0:T(1024)S(1)} %bitcast.206, f32[1024]{0:T(1024)S(1)} %bitcast.186, ...), kind=kOutput, calls=%fused_computation.23 | convolution fusion | flops 4045406208 | bytes 11547648 | tf_op jit(solution)/shard_map/dot_general | solution.py:55
  378.6 8.9 fusion.50
  389.8 106.1 %reduce-scatter.21.cloned.1.call-done = bf16[64,4096]{1,0:T(8,128)(2,1)} async-done(((bf16[1024,4096]{1,0:T(8,128)(2,1)}), bf16[64,4096]{1,0:T(8,128)(2,1)}) %reduce-scatter.21.cloned.1.call-update) | async-done | bytes 524304 | tf_op jit(solution)/shard_map/reduce_scatter | solution.py:229
  495.9 107.2 %reduce-scatter.23.cloned.1.call-done = bf16[256,1024]{1,0:T(8,128)(2,1)} async-done(((bf16[4096,1024]{1,0:T(8,128)(2,1)}), bf16[256,1024]{1,0:T(8,128)(2,1)}) %reduce-scatter.23.cloned.1.call-update) | async-done | bytes 524304 | tf_op jit(solution)/shard_map/reduce_scatter | solution.py:232
  603.1 88.6 %reduce-scatter.17.cloned.1.call-done = bf16[64,3072]{1,0:T(8,128)(2,1)} async-done(((bf16[1024,3072]{1,0:T(8,128)(2,1)}), bf16[64,3072]{1,0:T(8,128)(2,1)}) %reduce-scatter.17.cloned.1.call-update) | async-done | bytes 393232 | tf_op jit(solution)/shard_map/reduce_scatter | solution.py:223
  691.7 106.7 %reduce-scatter.15.cloned.1.call-done = bf16[64,4096]{1,0:T(8,128)(2,1)} async-done(((bf16[1024,4096]{1,0:T(8,128)(2,1)}), bf16[64,4096]{1,0:T(8,128)(2,1)}) %reduce-scatter.15.cloned.1.call-update) | async-done | bytes 524304 | tf_op jit(solution)/shard_map/reduce_scatter | solution.py:217
  798.4 10.8 %fusion.38 = bf16[1,640,1024]{2,1,0:T(8,128)(2,1)} fusion(f32[1,640,1024]{2,1,0:T(8,128)} %copy-done.9, bf16[640,4096]{1,0:T(8,128)(2,1)} %get-tuple-element.37, bf16[4096,1024]{1,0:T(8,128)(2,1)} %param.21), kind=kOutput, calls=%fused_computation.60 | convolution fusion | flops 5370019840 | bytes 17563648 | tf_op jit(solution)/shard_map/dot_general | solution.py:40
  809.2 32.7 %all-reduce = bf16[4096]{0:T(1024)(128)(2,1)S(1)} all-reduce(bf16[4096]{0:T(1024)(128)(2,1)S(1)} %convert_element_type.227), channel_id=6, replica_groups=mesh['items'=16,'seq'=2] {'items'}, use_global_device_ids=true, to_apply=%region_21.22.clone | all-reduce | flops 4096 | bytes 16384
  845.9 11.9 %reduce-scatter.29.cloned.1.call-done = bf16[64,8]{1,0:T(8,128)(2,1)} async-done(((bf16[1024,8]{1,0:T(8,128)(2,1)}), bf16[64,8]{1,0:T(8,128)(2,1)}) %reduce-scatter.29.cloned.1.call-update) | async-done | bytes 1040
  864.6 57.8 %all-reduce.5.cloned.1.call-done = (bf16[64,4096]{1,0:T(8,128)(2,1)}, bf16[64,3072]{1,0:T(8,128)(2,1)}, bf16[64,1024]{1,0:T(8,128)(2,1)}, bf16[64,4096]{1,0:T(8,128)(2,1)}, bf16[256,1024]{1,0:T(8,128)(2,1)}) async-done(((bf16[64,4096]{1,0:T(8,128)(2,1)}, bf16[64,3072]{1,0:T(8,128)(2,1)}, bf16[64,1024]{1,0:T(8,128)(2,1)}, bf16[64,4096]{1,0:T(8,128)(2,1)}, bf16[256,1024]{1,0:T(8,128)(2,1)}), ...) | async-done | bytes 2097168 | tf_op jit(solution)/shard_map/psum | solution.py:238
  (157 shorter events, 124.9 us)
Async XLA Ops:
  7.2 128.1 %copy-start = (bf16[1024,1024]{1,0:T(8,128)(2,1)S(1)}, bf16[1024,1024]{1,0:T(8,128)(2,1)}, u32[]{:S(2)}) copy-start(bf16[1024,1024]{1,0:T(8,128)(2,1)} %param.19) | copy-start | bytes 6291460
  7.2 59.4 %all-gather.5.cloned.1.call-start = ((), (), s32[]{:S(2)}) async-start(), calls=%async_computation.9 | async-start | bytes 3932160 | tf_op jit(solution)/shard_map/all_gather | solution.py:102
  9.6 8.1 copy-start.19
  9.6 8.1 slice-start.2
  24.7 83.9 %all-gather.3.cloned.1.call-start = ((), (), s32[]{:S(2)}) async-start(), calls=%async_computation.8 | async-start | bytes 3932160 | tf_op jit(solution)/shard_map/all_gather | solution.py:103
  25.4 306.2 %reduce-scatter.27.cloned.1.call-start = ((), (), s32[]{:S(2)}) async-start(), calls=%async_computation.16 | async-start | bytes 3932160
  28.3 42.7 %copy-start.2 = (bf16[1,640,1024]{1,2,0:T(8,128)(2,1)}, bf16[1,640,1024]{1,2,0:T(8,128)(2,1)S(1)}, u32[]{:S(2)}) copy-start(bf16[1,640,1024]{1,2,0:T(8,128)(2,1)S(1)} %copy.35) | copy-start | bytes 3932164
  113.0 22.3 %copy-start.5 = (bf16[1,640,1024]{2,1,0:T(8,128)(2,1)S(1)}, bf16[1,640,1024]{2,1,0:T(8,128)(2,1)}, u32[]{:S(2)}) copy-start(bf16[1,640,1024]{2,1,0:T(8,128)(2,1)} %param.11) | copy-start | bytes 3932164
  137.0 35.6 %copy-start.9 = (f32[1,640,1024]{2,1,0:T(8,128)}, f32[1,640,1024]{2,1,0:T(8,128)S(1)}, u32[]{:S(2)}) copy-start(f32[1,640,1024]{2,1,0:T(8,128)S(1)} %get-tuple-element.36) | copy-start | bytes 7864324
  137.4 12.4 %copy-start.13 = (bf16[1,640,1024]{2,1,0:T(8,128)(2,1)S(1)}, bf16[1,640,1024]{2,1,0:T(8,128)(2,1)}, u32[]{:S(2)}) copy-start(bf16[1,640,1024]{2,1,0:T(8,128)(2,1)} %param.12) | copy-start | bytes 3932164
  137.4 26.4 %slice-start = ((s8[8388608]{0:T(1024)(128)(4,1)}), s8[4194304]{0:T(1024)(128)(4,1)S(1)}, s32[]{:S(2)}) async-start(s8[8388608]{0:T(1024)(128)(4,1)} %bitcast.209), calls=%async_computation.19 | async-start | bytes 8388608
  149.8 14.0 %slice-start.1 = ((s8[8388608]{0:T(1024)(128)(4,1)}), s8[4194304]{0:T(1024)(128)(4,1)S(1)}, s32[]{:S(2)}) async-start(s8[8388608]{0:T(1024)(128)(4,1)} %bitcast.209), calls=%async_computation.20 | async-start | bytes 8388608
  177.5 23.3 %copy-start.11 = (bf16[640,1024]{0,1:T(8,128)(2,1)}, bf16[640,1024]{0,1:T(8,128)(2,1)S(1)}, u32[]{:S(2)}) copy-start(bf16[640,1024]{0,1:T(8,128)(2,1)S(1)} %copy.37) | copy-start | bytes 3932164
  217.4 124.6 %reduce-scatter.25.cloned.1.call-start = ((), (), s32[]{:S(2)}) async-start(), calls=%async_computation.15 | async-start | bytes 3932160
  221.2 33.9 %copy-start.3 = (bf16[1,640,1024]{1,2,0:T(8,128)(2,1)S(1)}, bf16[1,640,1024]{1,2,0:T(8,128)(2,1)}, u32[]{:S(2)}) copy-start(bf16[1,640,1024]{1,2,0:T(8,128)(2,1)} %copy-done.2) | copy-start | bytes 3932164
  286.3 103.5 %reduce-scatter.19.cloned.1.call-start = ((), (), s32[]{:S(2)}) async-start(), calls=%async_computation.12 | async-start | bytes 2228224 | tf_op jit(solution)/shard_map/reduce_scatter | solution.py:226
  292.4 203.5 %reduce-scatter.21.cloned.1.call-start = ((), (), s32[]{:S(2)}) async-start(), calls=%async_computation.13 | async-start | bytes 8912896 | tf_op jit(solution)/shard_map/reduce_scatter | solution.py:229
  304.7 298.4 %reduce-scatter.23.cloned.1.call-start = ((), (), s32[]{:S(2)}) async-start(), calls=%async_computation.14 | async-start | bytes 8912896 | tf_op jit(solution)/shard_map/reduce_scatter | solution.py:232
  317.5 374.2 %reduce-scatter.17.cloned.1.call-start = ((), (), s32[]{:S(2)}) async-start(), calls=%async_computation.11 | async-start | bytes 6684672 | tf_op jit(solution)/shard_map/reduce_scatter | solution.py:223
  362.4 436.0 %reduce-scatter.15.cloned.1.call-start = ((), (), s32[]{:S(2)}) async-start(), calls=%async_computation.10 | async-start | bytes 8912896 | tf_op jit(solution)/shard_map/reduce_scatter | solution.py:217
  378.5 479.3 %reduce-scatter.29.cloned.1.call-start = ((), (), s32[]{:S(2)}) async-start(), calls=%async_computation.17 | async-start | bytes 278528
  378.6 9.9 %copy-start.31 = (u32[32]{0:T(128)S(1)}, u32[32]{0:T(128)}, u32[]{:S(2)}) copy-start(u32[32]{0:T(128)} %constant.42) | copy-start | bytes 388
  388.4 534.0 %all-reduce.5.cloned.1.call-start = ((), (), s32[]{:S(2)}) async-start(), calls=%async_computation.18 | async-start | bytes 4194304 | tf_op jit(solution)/shard_map/psum | solution.py:238
  922.4 6.9 copy-start.15
  (23 other events, 103.6 us)
Sparse Core Ops, SparseCore 0:
  24.8 41.7 all-gather.4
  68.1 38.9 all-gather.2
  217.6 37.9 reduce-scatter.26
  286.4 37.7 reduce-scatter.24
  327.8 61.7 reduce-scatter.18
  393.5 102.3 reduce-scatter.20
  500.0 103.0 reduce-scatter.22
  607.0 84.6 reduce-scatter.16
  695.8 102.5 reduce-scatter.14
  802.4 55.3 reduce-scatter.28
  860.3 62.0 all-reduce.4
where the time goes:
time: 943 us; the launch traced here: 937 us
  waiting for transfers between devices  517 us (55%)
  matrix products  242 us (26%)
  local copies, waits for them, and re-layouts  77.4 us (8%)
  other arithmetic  44.1 us (5%)
  blocking collectives  37.6 us (4%)
  between operations  16.7 us (2%)
    reduce_scatter x1, waiting for transfers between devices, per_device(): lax.psum_scatter(grad_w_down.astype(jnp.bfloat16), 'items', scatter_dimen...  107 us
    reduce_scatter x1, waiting for transfers between devices, per_device(): lax.psum_scatter(grad_ada.astype(jnp.bfloat16), 'items', scatter_dimensio...  107 us
    reduce_scatter x1, waiting for transfers between devices, per_device(): lax.psum_scatter(grad_w_up.astype(jnp.bfloat16), 'items', scatter_dimensi...  106 us
    reduce_scatter x1, waiting for transfers between devices, per_device(): lax.psum_scatter(grad_w_qkv.astype(jnp.bfloat16), 'items', scatter_dimens...  88.6 us
    unnamed x84, local copies, waits for them, and re-layouts  62.1 us
    psum x1, waiting for transfers between devices, per_device(): lax.psum(parts[1].astype(jnp.bfloat16), 'seq').astype(jnp.float32)  57.8 us
    dot_general x4, matrix products, outer_sum(): lax.dot_general(left_flat, right_flat, (((0,), (0,)), ((), ())), preferre...  38.4 us
    all_gather x1, waiting for transfers between devices, per_device(): key_piece = lax.all_gather(key_local, 'seq', axis=1, tiled=True)  38.2 us
  transfers between devices with their start and end apart: 11, of which 7 were waited for; matrix products, arithmetic and copies ran while one was open for 24% of the time, Pallas kernels for 0%

commit v1 on v0

--- a/solution.py
+++ b/solution.py
@@ -2,6 +2,7 @@
 import jax.numpy as jnp
 from jax import lax
 from jax.sharding import PartitionSpec as P
+from jax.lax import all_gather
 
 HEADS = 16
 EPS = 1e-05
@@ -99,8 +100,13 @@
         return valid[:, None, None, :]
 
     run_max = jnp.full((group_count, head_count, row_count), NEGATIVE, jnp.float32)
-    key_piece = lax.all_gather(key_local, "seq", axis=1, tiled=True)
-    value_piece = lax.all_gather(value_local, "seq", axis=1, tiled=True)
+    key_piece, value_piece = jnp.split(
+        all_gather(
+            jnp.concatenate([key_local, value_local], axis=0), axis_name="seq", axis=1, tiled=True
+        ),
+        [key_local.shape[0]],
+        axis=0,
+    )
     count = key_piece.shape[1]
     key_heads = key_piece.reshape(group_count, count, head_count, head_size)
     value_heads = value_piece.reshape(group_count, count, head_count, head_size)

time: 943 us -> 1070 us (1.13)
  waiting for transfers between devices: 517 us -> 593 us
  matrix products: 242 us -> 276 us
  local copies, waits for them, and re-layouts: 77.4 us -> 93 us
    all_gather x0 -> x1, waiting for transfers between devices: none -> 42.6 us  [per_device(): all_gather(jnp.concatenate([key_local, value_local], axis=0), axis_name='...]
    all_gather x1, waiting for transfers between devices: 0.02 us -> 34.7 us  [per_device(): value_piece = lax.all_gather(value_local, 'seq', axis=1, tiled=True)]
    dot_general x1 -> x2, matrix products: 20.5 us -> 43.2 us  [per_device(): jnp.einsum('grhd,gkhd->ghrk', query_heads, key_heads, preferred_element_t...]
    split x0 -> x3, local copies, waits for them, and re-layouts: none -> 14.3 us  [per_device(): jnp.split(all_gather(jnp.concatenate([key_local, value_local], axis=0), a...]
    dot_general x4, matrix products: 29.6 us -> 42 us  [project(): result = jnp.dot(flat, weight, preferred_element_type=jnp.float32)]
    unnamed x84 -> x88, local copies, waits for them, and re-layouts: 62.1 us -> 63.1 us
  transfers between devices with their start and end apart: 11 -> 12, of which waited for: 7 -> 9; matrix products, arithmetic and copies ran while one was open for 24% -> 21% of each run, Pallas kernels for 0% -> 0%
where the time goes in v1:
time: 1070 us; the launch traced here: 1060 us
  waiting for transfers between devices  593 us (55%)
  matrix products  276 us (26%)
  local copies, waits for them, and re-layouts  93 us (9%)
  other arithmetic  47.3 us (4%)
  blocking collectives  37.5 us (4%)
  between operations  17.1 us (2%)
    reduce_scatter x1, waiting for transfers between devices, per_device(): lax.psum_scatter(grad_w_down.astype(jnp.bfloat16), 'items', scatter_dimen...  107 us
    reduce_scatter x1, waiting for transfers between devices, per_device(): lax.psum_scatter(grad_ada.astype(jnp.bfloat16), 'items', scatter_dimensio...  107 us
    reduce_scatter x1, waiting for transfers between devices, per_device(): lax.psum_scatter(grad_w_up.astype(jnp.bfloat16), 'items', scatter_dimensi...  106 us
    reduce_scatter x1, waiting for transfers between devices, per_device(): lax.psum_scatter(grad_w_qkv.astype(jnp.bfloat16), 'items', scatter_dimens...  88.7 us
    unnamed x88, local copies, waits for them, and re-layouts  63.1 us
    psum x1, waiting for transfers between devices, per_device(): lax.psum(parts[1].astype(jnp.bfloat16), 'seq').astype(jnp.float32)  57.7 us
    dot_general x2, matrix products, per_device(): jnp.einsum('grhd,gkhd->ghrk', query_heads, key_heads, preferred_element_t...  43.2 us
    all_gather x1, waiting for transfers between devices, per_device(): all_gather(jnp.concatenate([key_local, value_local], axis=0), axis_name='...  42.6 us
  transfers between devices with their start and end apart: 12, of which 9 were waited for; matrix products, arithmetic and copies ran while one was open for 21% of the time, Pallas kernels for 0%

profile of v1, /device:TPU:0, one launch (start us, length us, event | category | flops | bytes accessed | tf_op | source)
XLA Modules:
  0.0 1063.9 jit_solution(12498574730431113425)
XLA Ops:
  31.8 34.7 %all-gather.8.cloned.1.call-done = bf16[1,1280,1024]{2,1,0:T(8,128)(2,1)} async-done(((bf16[1,640,1024]{2,1,0:T(8,128)(2,1)}), bf16[1,1280,1024]{2,1,0:T(8,128)(2,1)}) %all-gather.8.cloned.1.call-update) | async-done | bytes 2621456 | tf_op jit(solution)/shard_map/all_gather | solution.py:157
  70.9 36.2 %all-gather.6.cloned.1.call-done = bf16[1,1280,1024]{2,1,0:T(8,128)(2,1)} async-done(((bf16[1,640,1024]{2,1,0:T(8,128)(2,1)}), bf16[1,1280,1024]{2,1,0:T(8,128)(2,1)}) %all-gather.6.cloned.1.call-update) | async-done | bytes 2621456 | tf_op jit(solution)/shard_map/all_gather | solution.py:156
  111.5 23.2 %fusion.79 = f32[16,640,1280]{2,1,0:T(8,128)} fusion(bf16[640,16,64]{0,2,1:T(8,128)(2,1)S(1)} %bitcast.166, bf16[1280,16,64]{0,2,1:T(8,128)(2,1)} %bitcast.164), kind=kOutput, calls=%fused_computation.122 | convolution fusion | flops 1677721600 | bytes 56360960 | tf_op jit(solution)/shard_map/grhd,gkhd->ghrk/dot_general | solution.py:163
  134.6 42.6 %all-gather.4.cloned.1.call-done = bf16[2,1280,1024]{2,1,0:T(8,128)(2,1)} async-done(((bf16[2,640,1024]{2,1,0:T(8,128)(2,1)}), bf16[2,1280,1024]{2,1,0:T(8,128)(2,1)}) %all-gather.4.cloned.1.call-update) | async-done | bytes 5242896 | tf_op jit(solution)/shard_map/all_gather | solution.py:104
  191.5 20.0 %fusion = (f32[16,640]{1,0:T(8,128)S(1)}, f32[16,640,1280]{2,1,0:T(8,128)}) fusion(pred[1280]{0:T(1024)(128)(4,1)S(1)} %fusion.53, bf16[640,16,64]{0,2,1:T(8,128)(2,1)S(1)} %bitcast.167, bf16[1280,16,64]{0,2,1:T(8,128)(2,1)} %bitcast.171), kind=kOutput, calls=%fused_computation.4 | convolution fusion | flops 1717032960 | bytes 56403200 | tf_op jit(solution)/shard_map/grhd,gkhd->ghrk/dot_general | solution.py:115
  211.5 17.2 %fusion.2 = f32[16,640]{1,0:T(8,128)S(1)} fusion(f32[16,640,1280]{2,1,0:T(8,128)} %get-tuple-element.34, f32[16,640]{1,0:T(8,128)S(1)} %broadcast_maximum_fusion, pred[1280]{0:T(1024)(128)(4,1)S(1)} %fusion.53), kind=kLoop, calls=%fused_computation.6 | loop fusion | flops 65525760 | bytes 52512000 | tf_op jit(solution)/shard_map/reduce_sum | solution.py:121
  228.8 20.5 %fusion.77 = (bf16[1,640,16,64]{1,3,2,0:T(8,128)(2,1)S(1)}, f32[1,640,16,64]{1,3,2,0:T(8,128)}) fusion(f32[640,16]{0,1:T(8,128)S(1)} %bitcast.184, bf16[1280,16,64]{0,2,1:T(8,128)(2,1)S(1)} %bitcast.177, f32[16,640,1280]{2,1,0:T(8,128)} %get-tuple-element.34, f32[16,640]{1,0:T(8,128)S(1)} %broadcast_maximum_fusion, pred[1280]{0:T(1024)(128)(4,1)S(1)} %fusion.53), kind=kOutput, calls=%fused_computation.120 | convolution fusion | flops 1744568320 | bytes 59065600 | tf_op jit(solution)/shard_map/ghrk,gkhd->grhd/dot_general | solution.py:122
  251.5 24.6 %multiply_convert_fusion.2 = (bf16[640,4096]{1,0:T(8,128)(2,1)}, f32[640,4096]{1,0:T(8,128)}) fusion(bf16[1024,4096]{1,0:T(8,128)(2,1)} %param.20, f32[1,640,1024]{2,1,0:T(8,128)S(1)} %get-tuple-element.38, f32[1024]{0:T(1024)S(1)} %bitcast.213, f32[1024]{0:T(1024)S(1)} %bitcast.196, f32[640]{0:T(1024)S(1)} %add_rsqrt_fusion, ...), kind=kOutput, calls=%fused_computation.20 | convolution fusion | flops 5385093120 | bytes 26752000 | tf_op jit(solution)/shard_map/dot_general | solution.py:41
  276.1 13.8 %fusion.15 = bf16[640,4096]{1,0:T(8,128)(2,1)} fusion(f32[640,4096]{1,0:T(8,128)} %get-tuple-element.40, bf16[4096,1024]{1,0:T(8,128)(2,1)} %param.21, bf16[1,640,1024]{2,1,0:T(8,128)(2,1)S(1)} %copy-done.15), kind=kOutput, calls=%fused_computation.19 | convolution fusion | flops 5394923520 | bytes 25427968 | tf_op jit(solution)/shard_map/dot_general | solution.py:47
  305.5 21.4 %fusion.17 = bf16[16,64,1280]{2,1,0:T(8,128)(2,1)} fusion(bf16[640,16,64]{0,2,1:T(8,128)(2,1)S(1)} %bitcast.181, f32[16,640,1280]{2,1,0:T(8,128)} %fusion.79, f32[16,640]{1,0:T(8,128)S(1)} %log_add_fusion, pred[1280]{0:T(1024)(128)(4,1)S(1)} %fusion.53), kind=kOutput, calls=%fused_computation.32 | convolution fusion | flops 1731461120 | bytes 56403200 | tf_op jit(solution)/shard_map/ghrk,grhd->gkhd/dot_general | solution.py:167
  326.9 11.5 %copy.47 = bf16[1,1280,1024]{2,0,1:T(2,128)(2,1)} copy(bf16[1,1280,1024]{1,2,0:T(8,128)(2,1)} %bitcast.178) | data formatting | bytes 5242880
  347.3 34.2 %multiply_convert_fusion = bf16[16,640,1280]{2,1,0:T(8,128)(2,1)} fusion(f32[16,640,1280]{2,1,0:T(8,128)} %fusion.79, bf16[640,16,64]{0,2,1:T(8,128)(2,1)S(1)} %bitcast.182, bf16[1280,16,64]{0,2,1:T(8,128)(2,1)S(1)} %bitcast.176, f32[16,640]{1,0:T(8,128)S(1)} %bitcast.190, f32[16,640]{1,0:T(8,128)S(1)} %log_add_fusion, pred[1280]{0:T(1024)(128)(4,1)S(1)} %fusion.53), kind=kOutput, calls=%fused_computation | convolution fusion | flops 1756364800 | bytes 82658560 | tf_op jit(solution)/shard_map/grhd,gkhd->ghrk/dot_general | solution.py:173
  381.5 14.6 %multiply_convert_fusion.3 = bf16[16,64,1280]{2,1,0:T(8,128)(2,1)} fusion(bf16[640,16,64]{0,2,1:T(8,128)(2,1)S(1)} %bitcast.168, bf16[16,640,1280]{2,1,0:T(8,128)(2,1)} %multiply_convert_fusion), kind=kOutput, calls=%fused_computation.25 | convolution fusion | flops 1680343040 | bytes 30146560 | tf_op jit(solution)/shard_map/ghrk,grhd->gkhd/dot_general | solution.py:182
  396.1 11.6 %copy.45 = bf16[1,1280,1024]{2,0,1:T(2,128)(2,1)} copy(bf16[1,1280,1024]{1,2,0:T(8,128)(2,1)} %bitcast.172) | data formatting | bytes 5242880
  418.9 12.2 %convolution_convert_fusion = bf16[1024,4096]{1,0:T(8,128)(2,1)} fusion(bf16[640,4096]{1,0:T(8,128)(2,1)} %fusion.15, f32[1,640,1024]{2,1,0:T(8,128)} %copy-done.10, f32[1024]{0:T(1024)S(1)} %bitcast.214, f32[1024]{0:T(1024)S(1)} %bitcast.200, f32[640]{0:T(1024)S(1)} %add_rsqrt_fusion, f32[640]{0:T(1024)S(1)} %broadcast_multiply_fusion.4), kind=kOutput, calls=%fused_computation.22 | convolution fusion | flops 5376180224 | bytes 16266240 | tf_op jit(solution)/shard_map/dot_general | solution.py:56
  432.4 11.5 %convolution_convert_fusion.1 = bf16[4096,1024]{1,0:T(8,128)(2,1)} fusion(bf16[640,4096]{1,0:T(8,128)(2,1)} %get-tuple-element.39, bf16[1,640,1024]{2,1,0:T(8,128)(2,1)S(1)} %copy-done.16), kind=kOutput, calls=%fused_computation.23 | convolution fusion | flops 5372903424 | bytes 14942208 | tf_op jit(solution)/shard_map/dot_general | solution.py:56
  444.0 14.1 %multiply_convert_fusion.4 = bf16[16,64,640]{2,1,0:T(8,128)(2,1)S(1)} fusion(bf16[1280,16,64]{0,2,1:T(8,128)(2,1)} %bitcast.165, bf16[16,640,1280]{2,1,0:T(8,128)(2,1)} %multiply_convert_fusion), kind=kOutput, calls=%fused_computation.63 | convolution fusion | flops 1679032320 | bytes 30146560 | tf_op jit(solution)/shard_map/ghrk,gkhd->grhd/dot_general | solution.py:178
  516.2 106.2 %reduce-scatter.21.cloned.1.call-done = bf16[64,4096]{1,0:T(8,128)(2,1)} async-done(((bf16[1024,4096]{1,0:T(8,128)(2,1)}), bf16[64,4096]{1,0:T(8,128)(2,1)}) %reduce-scatter.21.cloned.1.call-update) | async-done | bytes 524304 | tf_op jit(solution)/shard_map/reduce_scatter | solution.py:235
  622.4 107.2 %reduce-scatter.23.cloned.1.call-done = bf16[256,1024]{1,0:T(8,128)(2,1)} async-done(((bf16[4096,1024]{1,0:T(8,128)(2,1)}), bf16[256,1024]{1,0:T(8,128)(2,1)}) %reduce-scatter.23.cloned.1.call-update) | async-done | bytes 524304 | tf_op jit(solution)/shard_map/reduce_scatter | solution.py:238
  729.6 88.7 %reduce-scatter.17.cloned.1.call-done = bf16[64,3072]{1,0:T(8,128)(2,1)} async-done(((bf16[1024,3072]{1,0:T(8,128)(2,1)}), bf16[64,3072]{1,0:T(8,128)(2,1)}) %reduce-scatter.17.cloned.1.call-update) | async-done | bytes 393232 | tf_op jit(solution)/shard_map/reduce_scatter | solution.py:229
  818.2 106.5 %reduce-scatter.15.cloned.1.call-done = bf16[64,4096]{1,0:T(8,128)(2,1)} async-done(((bf16[1024,4096]{1,0:T(8,128)(2,1)}), bf16[64,4096]{1,0:T(8,128)(2,1)}) %reduce-scatter.15.cloned.1.call-update) | async-done | bytes 524304 | tf_op jit(solution)/shard_map/reduce_scatter | solution.py:223
  935.6 32.6 %all-reduce = bf16[4096]{0:T(1024)(128)(2,1)S(1)} all-reduce(bf16[4096]{0:T(1024)(128)(2,1)S(1)} %convert_element_type.227), channel_id=6, replica_groups=mesh['items'=16,'seq'=2] {'items'}, use_global_device_ids=true, to_apply=%region_21.22.clone | all-reduce | flops 4096 | bytes 16384
  972.2 12.1 %reduce-scatter.29.cloned.1.call-done = bf16[64,8]{1,0:T(8,128)(2,1)} async-done(((bf16[1024,8]{1,0:T(8,128)(2,1)}), bf16[64,8]{1,0:T(8,128)(2,1)}) %reduce-scatter.29.cloned.1.call-update) | async-done | bytes 1040
  991.2 57.7 %all-reduce.5.cloned.1.call-done = (bf16[64,4096]{1,0:T(8,128)(2,1)}, bf16[64,3072]{1,0:T(8,128)(2,1)}, bf16[64,1024]{1,0:T(8,128)(2,1)}, bf16[64,4096]{1,0:T(8,128)(2,1)}, bf16[256,1024]{1,0:T(8,128)(2,1)}) async-done(((bf16[64,4096]{1,0:T(8,128)(2,1)}, bf16[64,3072]{1,0:T(8,128)(2,1)}, bf16[64,1024]{1,0:T(8,128)(2,1)}, bf16[64,4096]{1,0:T(8,128)(2,1)}, bf16[256,1024]{1,0:T(8,128)(2,1)}), ...) | async-done | bytes 2097168 | tf_op jit(solution)/shard_map/psum | solution.py:244
  (169 shorter events, 172.1 us)
Async XLA Ops:
  7.2 242.2 %copy-start = (bf16[1024,1024]{1,0:T(8,128)(2,1)S(1)}, bf16[1024,1024]{1,0:T(8,128)(2,1)}, u32[]{:S(2)}) copy-start(bf16[1024,1024]{1,0:T(8,128)(2,1)} %param.19) | copy-start | bytes 6291460
  7.2 59.3 %all-gather.8.cloned.1.call-start = ((), (), s32[]{:S(2)}) async-start(), calls=%async_computation.10 | async-start | bytes 3932160 | tf_op jit(solution)/shard_map/all_gather | solution.py:157
  9.6 8.1 slice-start.2
  24.6 82.4 %all-gather.6.cloned.1.call-start = ((), (), s32[]{:S(2)}) async-start(), calls=%async_computation.9 | async-start | bytes 3932160 | tf_op jit(solution)/shard_map/all_gather | solution.py:156
  25.4 151.8 %all-gather.4.cloned.1.call-start = ((), (), s32[]{:S(2)}) async-start(), calls=%async_computation.8 | async-start | bytes 7864320 | tf_op jit(solution)/shard_map/all_gather | solution.py:104
  29.0 429.1 %reduce-scatter.27.cloned.1.call-start = ((), (), s32[]{:S(2)}) async-start(), calls=%async_computation.17 | async-start | bytes 3932160
  31.8 159.7 %copy-start.2 = (bf16[1,640,1024]{1,2,0:T(8,128)(2,1)}, bf16[1,640,1024]{1,2,0:T(8,128)(2,1)S(1)}, u32[]{:S(2)}) copy-start(bf16[1,640,1024]{1,2,0:T(8,128)(2,1)S(1)} %copy.39) | copy-start | bytes 3932164
  211.5 17.3 %copy-start.12 = (bf16[1,1280,1024]{1,2,0:T(8,128)(2,1)S(1)}, bf16[1,1280,1024]{1,2,0:T(8,128)(2,1)}, u32[]{:S(2)}) copy-start(bf16[1,1280,1024]{1,2,0:T(8,128)(2,1)} %copy.38) | copy-start | bytes 7864324
  228.8 20.5 %copy-start.5 = (bf16[1,640,1024]{2,1,0:T(8,128)(2,1)S(1)}, bf16[1,640,1024]{2,1,0:T(8,128)(2,1)}, u32[]{:S(2)}) copy-start(bf16[1,640,1024]{2,1,0:T(8,128)(2,1)} %param.11) | copy-start | bytes 3932164
  251.0 47.7 %copy-start.10 = (f32[1,640,1024]{2,1,0:T(8,128)}, f32[1,640,1024]{2,1,0:T(8,128)S(1)}, u32[]{:S(2)}) copy-start(f32[1,640,1024]{2,1,0:T(8,128)S(1)} %get-tuple-element.38) | copy-start | bytes 7864324
  251.5 24.7 %copy-start.15 = (bf16[1,640,1024]{2,1,0:T(8,128)(2,1)S(1)}, bf16[1,640,1024]{2,1,0:T(8,128)(2,1)}, u32[]{:S(2)}) copy-start(bf16[1,640,1024]{2,1,0:T(8,128)(2,1)} %param.12) | copy-start | bytes 3932164
  251.5 38.4 %slice-start = ((s8[8388608]{0:T(1024)(128)(4,1)}), s8[4194304]{0:T(1024)(128)(4,1)S(1)}, s32[]{:S(2)}) async-start(s8[8388608]{0:T(1024)(128)(4,1)} %bitcast.215), calls=%async_computation.20 | async-start | bytes 8388608
  276.1 13.8 %slice-start.1 = ((s8[8388608]{0:T(1024)(128)(4,1)}), s8[4194304]{0:T(1024)(128)(4,1)S(1)}, s32[]{:S(2)}) async-start(s8[8388608]{0:T(1024)(128)(4,1)} %bitcast.215), calls=%async_computation.21 | async-start | bytes 8388608
  303.6 23.3 %copy-start.13 = (bf16[640,1024]{0,1:T(8,128)(2,1)}, bf16[640,1024]{0,1:T(8,128)(2,1)S(1)}, u32[]{:S(2)}) copy-start(bf16[640,1024]{0,1:T(8,128)(2,1)S(1)} %copy.42) | copy-start | bytes 3932164
  343.6 124.9 %reduce-scatter.25.cloned.1.call-start = ((), (), s32[]{:S(2)}) async-start(), calls=%async_computation.16 | async-start | bytes 3932160
  347.3 34.2 %copy-start.3 = (bf16[1,640,1024]{1,2,0:T(8,128)(2,1)S(1)}, bf16[1,640,1024]{1,2,0:T(8,128)(2,1)}, u32[]{:S(2)}) copy-start(bf16[1,640,1024]{1,2,0:T(8,128)(2,1)} %copy-done.2) | copy-start | bytes 3932164
  412.7 103.5 %reduce-scatter.19.cloned.1.call-start = ((), (), s32[]{:S(2)}) async-start(), calls=%async_computation.13 | async-start | bytes 2228224 | tf_op jit(solution)/shard_map/reduce_scatter | solution.py:232
  418.9 203.6 %reduce-scatter.21.cloned.1.call-start = ((), (), s32[]{:S(2)}) async-start(), calls=%async_computation.14 | async-start | bytes 8912896 | tf_op jit(solution)/shard_map/reduce_scatter | solution.py:235
  431.1 298.4 %reduce-scatter.23.cloned.1.call-start = ((), (), s32[]{:S(2)}) async-start(), calls=%async_computation.15 | async-start | bytes 8912896 | tf_op jit(solution)/shard_map/reduce_scatter | solution.py:238
  443.9 374.3 %reduce-scatter.17.cloned.1.call-start = ((), (), s32[]{:S(2)}) async-start(), calls=%async_computation.12 | async-start | bytes 6684672 | tf_op jit(solution)/shard_map/reduce_scatter | solution.py:229
  488.9 435.9 %reduce-scatter.15.cloned.1.call-start = ((), (), s32[]{:S(2)}) async-start(), calls=%async_computation.11 | async-start | bytes 8912896 | tf_op jit(solution)/shard_map/reduce_scatter | solution.py:223
  504.9 479.4 %reduce-scatter.29.cloned.1.call-start = ((), (), s32[]{:S(2)}) async-start(), calls=%async_computation.18 | async-start | bytes 278528
  505.0 9.9 copy-start.33
  514.9 533.9 %all-reduce.5.cloned.1.call-start = ((), (), s32[]{:S(2)}) async-start(), calls=%async_computation.19 | async-start | bytes 4194304 | tf_op jit(solution)/shard_map/psum | solution.py:244
  (26 other events, 119.9 us)
Sparse Core Ops, SparseCore 0:
  24.7 41.7 all-gather.7
  68.0 38.9 all-gather.5
  108.6 68.5 all-gather.3
  343.7 37.6 reduce-scatter.26
  412.8 37.6 reduce-scatter.24
  454.1 61.7 reduce-scatter.18
  520.0 102.3 reduce-scatter.20
  626.5 103.0 reduce-scatter.22
  733.5 84.6 reduce-scatter.16
  822.2 102.5 reduce-scatter.14
  928.9 55.3 reduce-scatter.28
  986.7 62.0 all-reduce.4
